TPU v7x, 32 devices: a whole 2x2x4 slice. The times are simulated.
32 devices in a mesh: space: 8 (over z, x), filt: 4 (over y, core).
Axes of the slice: x: 2, y: 2, z: 4, core: 2. Of those that a mesh axis runs over, the one named last changes fastest.
Arguments:
- inputs: bfloat16 [16, 4, 32, 512], P('space'), may hold values from -6 to 6
- pre_hidden: bfloat16 [16, 4, 32, 512], P('space'), may hold values from -6 to 6
- weight_one: bfloat16 [512, 3, 3, 3, 512], P(None, None, None, None, 'filt'), may hold values from -0.0546875 to 0.0546875
- weight_two: bfloat16 [512, 3, 3, 3, 512], P(None, None, None, None, 'filt'), may hold values from -0.0546875 to 0.0546875
- grad_out: bfloat16 [16, 4, 32, 512], P('space', None, None, 'filt'), may hold values from -6 to 6
Outputs:
- grad_inputs: bfloat16 [16, 4, 32, 512], P('space', 'filt')
- grad_one: float32 [512, 3, 3, 3, 512], P('space', None, None, None, 'filt')
- grad_two: float32 [512, 3, 3, 3, 512], P('space', None, None, None, 'filt')
All inputs are finite; a program needn't handle non-finite values.
Results may differ from a plain program's by a relative error of at most 0.0049.
Values may be sent and summed in bfloat16 or wider, within the bound.
A program may use at most 128 MiB of HBM per device.

v0:
```python
import math

import jax
import jax.numpy as jnp
from jax import lax
from jax.sharding import PartitionSpec as P

TAP_LIST = [
    (tap_depth, tap_row, tap_col)
    for tap_depth in range(3)
    for tap_row in range(3)
    for tap_col in range(3)
]


def with_halo(block, sides, width):
    for axis, dim in sides:
        count = lax.axis_size(axis)
        forward = [(i, i + 1) for i in range(count - 1)]
        backward = [(target, source) for source, target in forward]
        low = lax.ppermute(
            lax.slice_in_dim(block, block.shape[dim] - width, None, axis=dim), axis, forward
        )
        high = lax.ppermute(lax.slice_in_dim(block, 0, width, axis=dim), axis, backward)
        block = jnp.concatenate([low, block, high], axis=dim)
    return block


def window_at(padded, tap, planes, height, columns):
    return padded[
        2 - tap[0] : 2 - tap[0] + planes,
        2 - tap[1] : 2 - tap[1] + height,
        2 - tap[2] : 2 - tap[2] + columns,
        :,
    ]


def pad_sides(field):
    return jnp.pad(field, ((0, 0), (1, 1), (1, 1), (0, 0)))


def carry_back(padded, weight, planes, height, columns):
    channels = weight.shape[4]
    summed = jnp.zeros((planes * height * columns, weight.shape[0]), jnp.float32)
    for tap in TAP_LIST:
        window = window_at(padded, tap, planes, height, columns).reshape(-1, channels)
        summed = summed + lax.dot_general(
            window,
            weight[:, tap[0], tap[1], tap[2], :],
            (((1,), (1,)), ((), ())),
            preferred_element_type=jnp.float32,
        )
    return summed.reshape(planes, height, columns, weight.shape[0])


def weight_terms(source, padded, row_count, planes, height, columns, factor):
    channels = padded.shape[3]
    pieces = []
    for tap in TAP_LIST:
        window = window_at(padded, tap, planes, height, columns).reshape(-1, channels)
        pieces.append(
            lax.dot_general(
                source, window, (((0,), (0,)), ((), ())), preferred_element_type=jnp.float32
            )
        )
    return jnp.stack(pieces, axis=1).reshape(row_count, 3, 3, 3, channels) * factor


def shards(inputs, pre_hidden, weight_one, weight_two, grad_out):
    planes, height, columns, in_channels = inputs.shape
    mid_channels = pre_hidden.shape[3]
    voxel_local = planes * height * columns
    factor = 1.0 / math.sqrt(voxel_local * lax.axis_size("space"))
    out_pad = pad_sides(with_halo(grad_out, (("space", 0),), 1))
    activity = jnp.maximum(pre_hidden, jnp.zeros_like(pre_hidden)).reshape(
        voxel_local, mid_channels
    )
    source_in = inputs.reshape(voxel_local, in_channels)
    hidden_partial = carry_back(out_pad, weight_two, planes, height, columns)
    grad_hidden = lax.psum_scatter(hidden_partial, "filt", scatter_dimension=3, tiled=True)
    group_width = grad_hidden.shape[3]
    own_pre = lax.dynamic_slice_in_dim(
        pre_hidden, lax.axis_index("filt") * group_width, group_width, 3
    )
    grad_pre = jnp.where(own_pre > 0, grad_hidden, jnp.zeros_like(grad_hidden)).astype(jnp.bfloat16)
    pre_pad = pad_sides(with_halo(grad_pre, (("space", 0),), 1))
    input_partial = carry_back(pre_pad, weight_one, planes, height, columns)
    whole_sum = lax.psum(input_partial, "filt")
    row_share = height // lax.axis_size("filt")
    grad_rows = lax.dynamic_slice_in_dim(
        whole_sum, lax.axis_index("filt") * row_share, row_share, 1
    )
    grad_inputs = grad_rows.astype(jnp.bfloat16)
    term_one = weight_terms(source_in, pre_pad, in_channels, planes, height, columns, factor)
    term_two = weight_terms(activity, out_pad, mid_channels, planes, height, columns, factor)
    grad_one, grad_two = (
        lax.psum_scatter(term_one, "space", scatter_dimension=0, tiled=True),
        lax.psum_scatter(term_two, "space", scatter_dimension=0, tiled=True),
    )
    return (grad_inputs, grad_one, grad_two)


def solution(mesh):
    placed = (
        P("space", None, None, None),
        P("space", None, None, None),
        P(None, None, None, None, "filt"),
        P(None, None, None, None, "filt"),
        P("space", None, None, "filt"),
    )
    return jax.shard_map(
        shards,
        mesh=mesh,
        in_specs=placed,
        out_specs=(
            P("space", "filt", None, None),
            P("space", None, None, None, "filt"),
            P("space", None, None, None, "filt"),
        ),
        check_vma=False,
    )
```

profile of v0, /device:TPU:0, one launch (start us, length us, event | category | flops | bytes accessed | tf_op | source)
XLA Modules:
  0.0 327.5 jit_solution(10588220274712867328)
XLA Ops:
  7.2 0.9 fusion.244
  8.2 5.0 %collective-permute-start = (bf16[1,4,32,128]{3,2,1,0:T(8,128)(2,1)S(1)}, bf16[1,4,32,128]{3,2,1,0:T(8,128)(2,1)S(1)}, u32[]{:S(2)}, u32[]{:S(2)}) collective-permute-start(bf16[1,4,32,128]{3,2,1,0:T(8,128)(2,1)S(1)} %get-tuple-element.57), channel_id=1, source_target_pairs={{0,4},{4,8},{8,12},{12,16},{16,20},{20,24},{24,28},{1,5},{5,9},{9,... | collective-permute-start | bytes 98312 | tf_op jit(solution)/shard_map/ppermute | solution.py:21
  13.2 1.3 collective-permute-start.1
  14.5 0.3 collective-permute-done
  14.8 4.2 %collective-permute-done.1 = bf16[1,4,32,128]{3,2,1,0:T(8,128)(2,1)S(1)} collective-permute-done((bf16[1,4,32,128]{3,2,1,0:T(8,128)(2,1)S(1)}, bf16[1,4,32,128]{3,2,1,0:T(8,128)(2,1)S(1)}, u32[]{:S(2)}, u32[]{:S(2)}) %collective-permute-start.1) | collective-permute-done | bytes 32800 | tf_op jit(solution)/shard_map/ppermute | solution.py:24
  19.0 0.9 fusion.68
  20.2 1.1 fusion.121
  21.3 1.1 fusion.127
  22.5 1.1 fusion.102
  23.6 1.1 convolution_add_fusion.47
  25.0 0.2 convolution_add_fusion.45
  29.3 0.2 fusion.1
  30.0 1.0 convolution_add_fusion.24
  37.3 3.8 %broadcast_multiply_fusion = f32[512,27,128]{0,2,1:T(8,128)} fusion(f32[512,27,128]{0,2,1:T(8,128)S(1)} %fusion.6), kind=kLoop, calls=%fused_computation | loop fusion | flops 1769472 | bytes 14155776 | tf_op jit(solution)/shard_map/mul | solution.py:66
  41.1 8.1 %copy.36 = f32[512,3,3,3,128]{4,0,3,2,1:T(8,128)} copy(f32[512,3,3,3,128]{0,4,3,2,1:T(8,128)} %bitcast.737) | data formatting | bytes 14155776 | tf_op jit(solution)/shard_map/mul | solution.py:66
  49.3 4.7 %reduce-scatter.4.cloned.1.call-done = f32[2,4,32,128]{3,2,1,0:T(8,128)} async-done(((f32[2,4,32,512]{3,2,1,0:T(8,128)}), f32[2,4,32,128]{3,2,1,0:T(8,128)}) %reduce-scatter.4.cloned.1.call-update) | async-done | bytes 131088 | tf_op jit(solution)/shard_map/reduce_scatter | solution.py:80
  54.0 0.9 select_convert_fusion
  55.0 3.4 %collective-permute-start.2 = (bf16[1,4,32,128]{3,2,1,0:T(8,128)(2,1)S(1)}, bf16[1,4,32,128]{3,2,1,0:T(8,128)(2,1)S(1)}, u32[]{:S(2)}, u32[]{:S(2)}) collective-permute-start(bf16[1,4,32,128]{3,2,1,0:T(8,128)(2,1)S(1)} %get-tuple-element.53), channel_id=1, source_target_pairs={{0,4},{4,8},{8,12},{12,16},{16,20},{20,24},{24,28},{1,5},{5,9},{9,... | collective-permute-start | bytes 98312 | tf_op jit(solution)/shard_map/ppermute | solution.py:21
  58.3 1.5 collective-permute-start.3
  59.9 4.2 %collective-permute-done.3 = bf16[1,4,32,128]{3,2,1,0:T(8,128)(2,1)S(1)} collective-permute-done((bf16[1,4,32,128]{3,2,1,0:T(8,128)(2,1)S(1)}, bf16[1,4,32,128]{3,2,1,0:T(8,128)(2,1)S(1)}, u32[]{:S(2)}, u32[]{:S(2)}) %collective-permute-start.3) | collective-permute-done | bytes 32800 | tf_op jit(solution)/shard_map/ppermute | solution.py:24
  70.0 3.7 %broadcast_multiply_fusion.1 = f32[512,27,128]{0,2,1:T(8,128)} fusion(f32[512,27,128]{0,2,1:T(8,128)S(1)} %fusion.33), kind=kLoop, calls=%fused_computation.1 | loop fusion | flops 1769472 | bytes 14155776 | tf_op jit(solution)/shard_map/mul | solution.py:66
  73.7 8.1 %copy.8 = f32[512,3,3,3,128]{4,0,3,2,1:T(8,128)} copy(f32[512,3,3,3,128]{0,4,3,2,1:T(8,128)} %bitcast.738) | data formatting | bytes 14155776 | tf_op jit(solution)/shard_map/mul | solution.py:66
  81.9 1.3 fusion.91
  83.2 1.1 fusion.97
  84.6 1.1 fusion.72
  85.7 1.1 convolution_add_fusion.23
  86.8 1.1 convolution_add_fusion.22
  88.2 0.2 fusion.2
  93.2 16.8 %all-reduce.3 = bf16[2,4,32,512]{3,2,1,0:T(8,128)(2,1)S(1)} all-reduce(f32[2,4,32,512]{3,2,1,0:T(8,128)S(1)} %bitcast.741), channel_id=1, replica_groups=mesh['space'=8,'filt'=4] {'filt'}, use_global_device_ids=true, to_apply=%region_1.2 | all-reduce | flops 131072 | bytes 786432 | tf_op jit(solution)/shard_map/psum | solution.py:88
  110.0 0.6 dynamic-slice_convert_fusion
  110.6 77.3 %reduce-scatter.8.cloned.1.call-done = f32[64,3,3,3,128]{4,0,3,2,1:T(8,128)} async-done(((f32[512,3,3,3,128]{4,0,3,2,1:T(8,128)}), f32[64,3,3,3,128]{4,0,3,2,1:T(8,128)}) %reduce-scatter.8.cloned.1.call-update) | async-done | bytes 884752 | tf_op jit(solution)/shard_map/reduce_scatter | solution.py:98
  187.9 133.0 %reduce-scatter.6.cloned.1.call-done = f32[64,3,3,3,128]{4,0,3,2,1:T(8,128)} async-done(((f32[512,3,3,3,128]{4,0,3,2,1:T(8,128)}), f32[64,3,3,3,128]{4,0,3,2,1:T(8,128)}) %reduce-scatter.6.cloned.1.call-update) | async-done | bytes 884752 | tf_op jit(solution)/shard_map/reduce_scatter | solution.py:97
  (120 shorter events, 21.9 us)
Async XLA Ops:
  7.2 57.1 %copy-start = (bf16[2,4,32,512]{3,2,1,0:T(8,128)(2,1)S(1)}, bf16[2,4,32,512]{3,2,1,0:T(8,128)(2,1)}, u32[]{:S(2)}) copy-start(bf16[2,4,32,512]{3,2,1,0:T(8,128)(2,1)} %param.5) | copy-start | bytes 786436
  7.2 18.0 %copy-start.4 = (bf16[2,4,32,128]{3,2,1,0:T(8,128)(2,1)S(1)}, bf16[2,4,32,128]{3,2,1,0:T(8,128)(2,1)}, u32[]{:S(2)}) copy-start(bf16[2,4,32,128]{3,2,1,0:T(8,128)(2,1)} %param.9) | copy-start | bytes 196612
  7.2 46.8 %reduce-scatter.4.cloned.1.call-start = ((), (), s32[]{:S(2)}) async-start(), calls=%async_computation.3 | async-start | bytes 655360 | tf_op jit(solution)/shard_map/reduce_scatter | solution.py:80
  7.2 17.5 %copy-start.2 = (bf16[512,3,3,3,128]{4,0,3,2,1:T(8,128)(2,1)S(1)}, bf16[512,3,3,3,128]{4,0,3,2,1:T(8,128)(2,1)}, u32[]{:S(2)}) copy-start(bf16[512,3,3,3,128]{4,0,3,2,1:T(8,128)(2,1)} %param.8) | copy-start | bytes 10616836
  8.2 6.6 %collective-permute-start = (bf16[1,4,32,128]{3,2,1,0:T(8,128)(2,1)S(1)}, bf16[1,4,32,128]{3,2,1,0:T(8,128)(2,1)S(1)}, u32[]{:S(2)}, u32[]{:S(2)}) collective-permute-start(bf16[1,4,32,128]{3,2,1,0:T(8,128)(2,1)S(1)} %get-tuple-element.57), channel_id=1, source_target_pairs={{0,4},{4,8},{8,12},{12,16},{16,20},{20,24},{24,28},{1,5},{5,9},{9,... | collective-permute-start | bytes 98312 | tf_op jit(solution)/shard_map/ppermute | solution.py:21
  13.2 5.8 %collective-permute-start.1 = (bf16[1,4,32,128]{3,2,1,0:T(8,128)(2,1)S(1)}, bf16[1,4,32,128]{3,2,1,0:T(8,128)(2,1)S(1)}, u32[]{:S(2)}, u32[]{:S(2)}) collective-permute-start(bf16[1,4,32,128]{3,2,1,0:T(8,128)(2,1)S(1)} %get-tuple-element.58), channel_id=1, source_target_pairs={{4,0},{8,4},{12,8},{16,12},{20,16},{24,20},{28,24},{5,1},{9,5},{13... | collective-permute-start | bytes 98312 | tf_op jit(solution)/shard_map/ppermute | solution.py:24
  27.8 3.2 copy-start.1
  31.0 156.9 %reduce-scatter.8.cloned.1.call-start = ((), (), s32[]{:S(2)}) async-start(), calls=%async_computation.5 | async-start | bytes 7962624 | tf_op jit(solution)/shard_map/reduce_scatter | solution.py:98
  49.2 271.7 %reduce-scatter.6.cloned.1.call-start = ((), (), s32[]{:S(2)}) async-start(), calls=%async_computation.4 | async-start | bytes 7962624 | tf_op jit(solution)/shard_map/reduce_scatter | solution.py:97
  55.0 5.0 %collective-permute-start.2 = (bf16[1,4,32,128]{3,2,1,0:T(8,128)(2,1)S(1)}, bf16[1,4,32,128]{3,2,1,0:T(8,128)(2,1)S(1)}, u32[]{:S(2)}, u32[]{:S(2)}) collective-permute-start(bf16[1,4,32,128]{3,2,1,0:T(8,128)(2,1)S(1)} %get-tuple-element.53), channel_id=1, source_target_pairs={{0,4},{4,8},{8,12},{12,16},{16,20},{20,24},{24,28},{1,5},{5,9},{9,... | collective-permute-start | bytes 98312 | tf_op jit(solution)/shard_map/ppermute | solution.py:21
  58.3 5.8 %collective-permute-start.3 = (bf16[1,4,32,128]{3,2,1,0:T(8,128)(2,1)S(1)}, bf16[1,4,32,128]{3,2,1,0:T(8,128)(2,1)S(1)}, u32[]{:S(2)}, u32[]{:S(2)}) collective-permute-start(bf16[1,4,32,128]{3,2,1,0:T(8,128)(2,1)S(1)} %get-tuple-element.54), channel_id=1, source_target_pairs={{4,0},{8,4},{12,8},{16,12},{20,16},{24,20},{28,24},{5,1},{9,5},{13... | collective-permute-start | bytes 98312 | tf_op jit(solution)/shard_map/ppermute | solution.py:24
  81.8 6.2 %copy-start.3 = (bf16[512,3,3,3,128]{4,0,3,2,1:T(8,128)(2,1)S(1)}, bf16[512,3,3,3,128]{4,0,3,2,1:T(8,128)(2,1)}, u32[]{:S(2)}) copy-start(bf16[512,3,3,3,128]{4,0,3,2,1:T(8,128)(2,1)} %param.7) | copy-start | bytes 10616836
Sparse Core Ops, SparseCore 0:
  31.2 22.8 reduce-scatter.3
  58.3 129.5 reduce-scatter.7
  192.2 128.7 reduce-scatter.5
where the time goes:
time: 328 us; the launch traced here: 327 us
  waiting for transfers between devices  224 us (68%)
  matrix products  33 us (10%)
  local copies, waits for them, and re-layouts  18.3 us (6%)
  blocking collectives  16.8 us (5%)
  between operations  14.8 us (5%)
  starting transfers between devices  11.3 us (3%)
  other arithmetic  9.44 us (3%)
    reduce_scatter x1, waiting for transfers between devices, shards(): lax.psum_scatter(term_one, 'space', scatter_dimension=0, tiled=True)  133 us
    reduce_scatter x1, waiting for transfers between devices, shards(): lax.psum_scatter(term_two, 'space', scatter_dimension=0, tiled=True)  77.3 us
    dot_general x54, matrix products, carry_back(): lax.dot_general(window, weight[:, tap[0], tap[1], tap[2], :], (((1,), (1,...  21.4 us
    psum x1, blocking collectives, shards(): whole_sum = lax.psum(input_partial, 'filt')  16.8 us
    mul x2, local copies, waits for them, and re-layouts, weight_terms(): jnp.stack(pieces, axis=1).reshape(row_count, 3, 3, 3, channels) * factor  16.2 us
    dot_general x54, matrix products, weight_terms(): lax.dot_general(source, window, (((0,), (0,)), ((), ())), preferred_eleme...  11.6 us
    ppermute x2, waiting for transfers between devices, with_halo(): lax.ppermute(lax.slice_in_dim(block, 0, width, axis=dim), axis, backward)  8.46 us
    ppermute x2, starting transfers between devices, with_halo(): lax.ppermute(lax.slice_in_dim(block, block.shape[dim] - width, None, axis...  8.37 us
  transfers between devices with their start and end apart: 7, of which 7 were waited for; matrix products, arithmetic and copies ran while one was open for 15% of the time, Pallas kernels for 0%

commit v1 on v0

v1 whole, which is shorter than its diff:
```python
import math

import jax
import jax.numpy as jnp
from jax import lax
from jax.sharding import PartitionSpec as P

TAP_LIST = [
    (tap_depth, tap_row, tap_col)
    for tap_depth in range(3)
    for tap_row in range(3)
    for tap_col in range(3)
]


def window_at(padded, tap, planes, height, columns):
    return padded[
        2 - tap[0] : 2 - tap[0] + planes,
        2 - tap[1] : 2 - tap[1] + height,
        2 - tap[2] : 2 - tap[2] + columns,
        :,
    ]


def carry_back(padded, weight, planes, height, columns):
    channels = weight.shape[4]
    summed = jnp.zeros((planes * height * columns, weight.shape[0]), jnp.float32)
    for tap in TAP_LIST:
        window = window_at(padded, tap, planes, height, columns).reshape(-1, channels)
        summed = summed + lax.dot_general(
            window,
            weight[:, tap[0], tap[1], tap[2], :],
            (((1,), (1,)), ((), ())),
            preferred_element_type=jnp.float32,
        )
    return summed.reshape(planes, height, columns, weight.shape[0])


def weight_terms(source, padded, planes, height, columns, factor):
    channels = padded.shape[3]
    pieces = []
    for tap in TAP_LIST:
        window = window_at(padded, tap, planes, height, columns).reshape(-1, channels)
        pieces.append(
            lax.dot_general(
                source, window, (((1,), (0,)), ((), ())), preferred_element_type=jnp.float32
            )
            * factor
        )
    return jnp.stack(pieces, axis=1).reshape(source.shape[0], 3, 3, 3, channels)


def pad_all(field):
    return jnp.pad(field, ((1, 1), (1, 1), (1, 1), (0, 0)))


def shards(inputs, pre_hidden, weight_one, weight_two, grad_out):
    planes, height, columns, in_channels = inputs.shape
    mid_channels = pre_hidden.shape[3]
    count = lax.axis_size("space")
    voxel_local = planes * height * columns
    factor = 1.0 / math.sqrt(voxel_local * count)
    start = lax.axis_index("space") * planes

    out_all = pad_all(lax.all_gather(grad_out, "space", axis=0, tiled=True))
    out_pad = lax.dynamic_slice_in_dim(out_all, start, planes + 2, 0)
    activity = jnp.maximum(pre_hidden, jnp.zeros_like(pre_hidden))
    both = jnp.stack([activity, inputs]).reshape(2, voxel_local, in_channels)
    both = jnp.swapaxes(both, 1, 2).reshape(2, count, in_channels // count, voxel_local)
    both = lax.all_to_all(both, "space", 1, 1)
    both = jnp.swapaxes(both, 1, 2).reshape(2, in_channels // count, count * voxel_local)

    hidden_partial = carry_back(out_pad, weight_two, planes, height, columns)
    grad_hidden = lax.psum_scatter(hidden_partial, "filt", scatter_dimension=3, tiled=True)
    group_width = grad_hidden.shape[3]
    own_pre = lax.dynamic_slice_in_dim(
        pre_hidden, lax.axis_index("filt") * group_width, group_width, 3
    )
    grad_pre = jnp.where(own_pre > 0, grad_hidden, jnp.zeros_like(grad_hidden)).astype(jnp.bfloat16)
    pre_all = pad_all(lax.all_gather(grad_pre, "space", axis=0, tiled=True))
    pre_pad = lax.dynamic_slice_in_dim(pre_all, start, planes + 2, 0)
    input_partial = carry_back(pre_pad, weight_one, planes, height, columns)
    grad_rows = lax.psum_scatter(input_partial, "filt", scatter_dimension=1, tiled=True)
    grad_inputs = grad_rows.astype(jnp.bfloat16)
    depth = planes * count
    grad_two = weight_terms(both[0], out_all, depth, height, columns, factor)
    grad_one = weight_terms(both[1], pre_all, depth, height, columns, factor)
    return (grad_inputs, grad_one, grad_two)


def solution(mesh):
    placed = (
        P("space", None, None, None),
        P("space", None, None, None),
        P(None, None, None, None, "filt"),
        P(None, None, None, None, "filt"),
        P("space", None, None, "filt"),
    )
    return jax.shard_map(
        shards,
        mesh=mesh,
        in_specs=placed,
        out_specs=(
            P("space", "filt", None, None),
            P("space", None, None, None, "filt"),
            P("space", None, None, None, "filt"),
        ),
        check_vma=False,
    )
```

time: 328 us -> 191 us (0.58)
  waiting for transfers between devices: 224 us -> 0.02 us
  blocking collectives: 16.8 us -> 87.4 us
  matrix products: 33 us -> 55.3 us
  other arithmetic: 9.44 us -> 2.93 us
  starting transfers between devices: 11.3 us -> 7.32 us
  local copies, waits for them, and re-layouts: 18.3 us -> 21.9 us
    reduce_scatter x2 -> x0, waiting for transfers between devices: 210 us -> none  [the longest x1 133 us: shards(): lax.psum_scatter(term_one, 'space', scatter_dimension=0, tiled=True)]
    all_gather x0 -> x2, blocking collectives: none -> 70 us  [the longest x1 38.5 us: shards(): out_all = pad_all(lax.all_gather(grad_out, 'space', axis=0, tiled=True))]
    dot_general x54, matrix products: 11.6 us -> 37.7 us  [weight_terms(): lax.dot_general(source, window, (((1,), (0,)), ((), ())), preferred_eleme...]
    unnamed x0 -> x1, blocking collectives: none -> 17.4 us
    psum x1 -> x0, blocking collectives: 16.8 us -> none  [shards(): whole_sum = lax.psum(input_partial, 'filt')]
    slice x4 -> x8, local copies, waits for them, and re-layouts: 0.54 us -> 16.7 us  [window_at(): padded[2 - tap[0]:2 - tap[0] + planes, 2 - tap[1]:2 - tap[1] + height, 2...]
    mul x2 -> x0, local copies, waits for them, and re-layouts: 16.2 us -> none  [weight_terms(): jnp.stack(pieces, axis=1).reshape(row_count, 3, 3, 3, channels) * factor]
    ppermute x4 -> x0, starting transfers between devices: 11.1 us -> none  [the longest x2 8.37 us: with_halo(): lax.ppermute(lax.slice_in_dim(block, block.shape[dim] - width, None, axis...]
  transfers between devices with their start and end apart: 7 -> 2, of which waited for: 7 -> 0; matrix products, arithmetic and copies ran while one was open for 15% -> 25% of each run, Pallas kernels for 0% -> 0%
where the time goes in v1:
time: 191 us; the launch traced here: 190 us
  blocking collectives  87.4 us (46%)
  matrix products  55.3 us (29%)
  local copies, waits for them, and re-layouts  21.9 us (11%)
  between operations  15 us (8%)
  starting transfers between devices  7.32 us (4%)
  other arithmetic  2.93 us (2%)
    all_gather x1, blocking collectives, shards(): out_all = pad_all(lax.all_gather(grad_out, 'space', axis=0, tiled=True))  38.5 us
    dot_general x54, matrix products, weight_terms(): lax.dot_general(source, window, (((1,), (0,)), ((), ())), preferred_eleme...  37.7 us
    all_gather x1, blocking collectives, shards(): pre_all = pad_all(lax.all_gather(grad_pre, 'space', axis=0, tiled=True))  31.5 us
    dot_general x54, matrix products, carry_back(): lax.dot_general(window, weight[:, tap[0], tap[1], tap[2], :], (((1,), (1,...  17.5 us
    unnamed x1, blocking collectives  17.4 us
    slice x8, local copies, waits for them, and re-layouts, window_at(): padded[2 - tap[0]:2 - tap[0] + planes, 2 - tap[1]:2 - tap[1] + height, 2...  16.7 us
    all_to_all x1, starting transfers between devices, shards(): both = lax.all_to_all(both, 'space', 1, 1)  7.28 us
  transfers between devices with their start and end apart: 2, of which 0 were waited for; matrix products, arithmetic and copies ran while one was open for 25% of the time, Pallas kernels for 0%

profile of v1, /device:TPU:0, one launch (start us, length us, event | category | flops | bytes accessed | tf_op | source)
XLA Modules:
  0.0 189.9 jit_solution(2208045454308915686)
XLA Ops:
  7.2 1.0 broadcast_maximum_fusion
  8.2 1.0 maximum_bitcast_fusion
  10.2 7.3 %all-to-all-start = ((bf16[2,8,64,256]{3,2,0,1:T(8,128)(2,1)}), bf16[2,8,64,256]{3,2,0,1:T(8,128)(2,1)}, u32[]{:S(2)}, u32[]{:S(2)}) async-start(bf16[2,8,64,256]{3,2,0,1:T(8,128)(2,1)} %copy.16), calls=%async_computation.1 | async-start | bytes 1048576 | tf_op jit(solution)/shard_map/all_to_all | solution.py:70
  17.6 38.5 %all_gather.6 = bf16[16,4,32,128]{3,2,1,0:T(8,128)(2,1)S(1)} all-gather(bf16[2,4,32,128]{3,2,1,0:T(8,128)(2,1)S(1)} %copy-done.36), channel_id=1, replica_groups=mesh['space'=8,'filt'=4] {'space'}, dimensions={0}, use_global_device_ids=true | all-gather | bytes 589824 | tf_op jit(solution)/shard_map/all_gather | solution.py:65
  56.9 1.0 pad_dynamic-slice_fusion.53
  57.9 1.1 fusion.162
  59.0 1.1 convolution_add_fusion.51
  60.1 1.1 convolution_add_fusion.50
  61.3 1.1 convolution_add_fusion.49
  67.6 1.0 convolution_add_fusion.26
  69.3 2.2 %pad_slice_fusion.27 = (bf16[16,4,32,128]{3,2,1,0:T(8,128)(2,1)}, bf16[16,4,32,128]{3,2,1,0:T(8,128)(2,1)}, bf16[16,4,32,128]{3,2,1,0:T(8,128)(2,1)}, bf16[16,4,...) fusion(bf16[16,4,32,128]{3,2,1,0:T(8,128)(2,1)S(1)} %all_gather.6), kind=kLoop, calls=%fused_computation.80 | loop fusion | bytes 4194304 | tf_op jit(solution)/shard_map/slice | solution.py:17
  71.5 4.4 %pad_slice_fusion.26 = (bf16[16,4,32,128]{3,2,1,0:T(8,128)(2,1)S(1)}, bf16[16,4,32,128]{3,2,1,0:T(8,128)(2,1)}, bf16[16,4,32,128]{3,2,1,0:T(8,128)(2,1)}, bf16[1...) fusion(bf16[16,4,32,128]{3,2,1,0:T(8,128)(2,1)S(1)} %all_gather.6), kind=kLoop, calls=%fused_computation.79 | loop fusion | bytes 10485760 | tf_op jit(solution)/shard_map/slice | solution.py:17
  75.9 1.2 fusion.218
  77.2 2.0 %fusion.53 = f32[64,27,128]{2,0,1:T(8,128)} fusion(bf16[64,2048]{1,0:T(8,128)(2,1)S(1)} %bitcast.700, bf16[2048,128]{1,0:T(8,128)(2,1)} %bitcast.766), kind=kOutput, calls=%fused_computation.238 | convolution fusion | flops 33562624 | bytes 819200 | tf_op jit(solution)/shard_map/dot_general | solution.py:45
  79.2 1.9 %fusion.51 = f32[64,27,128]{2,0,1:T(8,128)} fusion(f32[64,27,128]{2,0,1:T(8,128)} %fusion.53, bf16[64,2048]{1,0:T(8,128)(2,1)S(1)} %bitcast.701, bf16[2048,128]{1,0:T(8,128)(2,1)} %bitcast.765), kind=kOutput, calls=%fused_computation.235 | convolution fusion | flops 33562624 | bytes 819200 | tf_op jit(solution)/shard_map/dot_general | solution.py:45
  81.1 2.0 %fusion.49 = f32[64,27,128]{2,0,1:T(8,128)} fusion(f32[64,27,128]{2,0,1:T(8,128)} %fusion.51, bf16[64,2048]{1,0:T(8,128)(2,1)S(1)} %bitcast.702, bf16[2048,128]{1,0:T(8,128)(2,1)} %bitcast.764), kind=kOutput, calls=%fused_computation.232 | convolution fusion | flops 33562624 | bytes 819200 | tf_op jit(solution)/shard_map/dot_general | solution.py:45
  93.3 0.8 fusion.23
  95.0 0.9 fusion.19
  95.8 0.8 fusion.17
  103.4 0.9 select_convert_fusion
  104.4 31.5 %all_gather.7 = bf16[16,4,32,128]{3,2,1,0:T(8,128)(2,1)S(1)} all-gather(bf16[2,4,32,128]{3,2,1,0:T(8,128)(2,1)S(1)} %select_convert_fusion), channel_id=1, replica_groups=mesh['space'=8,'filt'=4] {'space'}, dimensions={0}, use_global_device_ids=true | all-gather | bytes 589824 | tf_op jit(solution)/shard_map/all_gather | solution.py:80
  135.8 4.5 %pad_slice_fusion = (bf16[16,4,32,128]{3,2,1,0:T(8,128)(2,1)S(1)}, bf16[16,4,32,128]{3,2,1,0:T(8,128)(2,1)}, bf16[16,4,32,128]{3,2,1,0:T(8,128)(2,1)}, bf16[16,4...) fusion(bf16[16,4,32,128]{3,2,1,0:T(8,128)(2,1)S(1)} %all_gather.7), kind=kLoop, calls=%fused_computation.26 | loop fusion | bytes 10485760 | tf_op jit(solution)/shard_map/slice | solution.py:17
  140.3 2.2 %pad_slice_fusion.1 = (bf16[16,4,32,128]{3,2,1,0:T(8,128)(2,1)}, bf16[16,4,32,128]{3,2,1,0:T(8,128)(2,1)}, bf16[16,4,32,128]{3,2,1,0:T(8,128)(2,1)}, bf16[16,4,3...) fusion(bf16[16,4,32,128]{3,2,1,0:T(8,128)(2,1)S(1)} %all_gather.7), kind=kLoop, calls=%fused_computation.27 | loop fusion | bytes 4194304 | tf_op jit(solution)/shard_map/slice | solution.py:17
  142.5 1.0 pad_dynamic-slice_fusion.26
  150.4 1.0 convolution_add_fusion
  151.4 17.4 %all-reduce.4 = bf16[2,4,32,512]{3,2,1,0:T(8,128)(2,1)} all-reduce(f32[2,4,32,512]{3,2,1,0:T(8,128)} %bitcast.768), channel_id=3, replica_groups=mesh['space'=8,'filt'=4] {'filt'}, use_global_device_ids=true, to_apply=%region_1.2.clone | all-reduce | flops 131072 | bytes 786432
  168.8 1.4 fusion.107
  170.3 1.3 fusion.105
  171.6 1.3 fusion.103
  172.9 1.3 fusion.101
  174.3 1.3 fusion.99
  180.9 2.1 %dynamic-slice_convert_fusion = bf16[2,1,32,512]{3,2,1,0:T(8,128)(2,1)} fusion(bf16[2,4,32,512]{3,2,1,0:T(8,128)(2,1)} %all-reduce.4, u32[]{:T(128)} %bitcast.231), kind=kLoop, calls=%fused_computation.321 | loop fusion | bytes 131076 | tf_op jit(solution)/shard_map/convert_element_type | solution.py:84
  (180 shorter events, 37.1 us)
Async XLA Ops:
  7.2 10.4 %copy-start.36 = (bf16[2,4,32,128]{3,2,1,0:T(8,128)(2,1)S(1)}, bf16[2,4,32,128]{3,2,1,0:T(8,128)(2,1)}, u32[]{:S(2)}) copy-start(bf16[2,4,32,128]{3,2,1,0:T(8,128)(2,1)} %param.9) | copy-start | bytes 196612
  10.2 65.7 %all-to-all-start = ((bf16[2,8,64,256]{3,2,0,1:T(8,128)(2,1)}), bf16[2,8,64,256]{3,2,0,1:T(8,128)(2,1)}, u32[]{:S(2)}, u32[]{:S(2)}) async-start(bf16[2,8,64,256]{3,2,0,1:T(8,128)(2,1)} %copy.16), calls=%async_computation.1 | async-start | bytes 1048576 | tf_op jit(solution)/shard_map/all_to_all | solution.py:70
  17.5 85.9 %reduce-scatter.5.cloned.1.call-start = ((), (), s32[]{:S(2)}) async-start(), calls=%async_computation.2 | async-start | bytes 655360 | tf_op jit(solution)/shard_map/reduce_scatter | solution.py:74
  56.1 6.3 %copy-start = (bf16[512,3,3,3,128]{4,0,3,2,1:T(8,128)(2,1)S(1)}, bf16[512,3,3,3,128]{4,0,3,2,1:T(8,128)(2,1)}, u32[]{:S(2)}) copy-start(bf16[512,3,3,3,128]{4,0,3,2,1:T(8,128)(2,1)} %param.8) | copy-start | bytes 10616836
  75.9 7.2 %copy-start.21 = (bf16[16,4,32,128]{3,2,1,0:T(8,128)(2,1)S(1)}, bf16[16,4,32,128]{3,2,1,0:T(8,128)(2,1)}, u32[]{:S(2)}) copy-start(bf16[16,4,32,128]{3,2,1,0:T(8,128)(2,1)} %get-tuple-element.7) | copy-start | bytes 1572868
  75.9 8.1 %copy-start.20 = (bf16[16,4,32,128]{3,2,1,0:T(8,128)(2,1)S(1)}, bf16[16,4,32,128]{3,2,1,0:T(8,128)(2,1)}, u32[]{:S(2)}) copy-start(bf16[16,4,32,128]{3,2,1,0:T(8,128)(2,1)} %get-tuple-element.8) | copy-start | bytes 1572868
  75.9 8.9 %copy-start.19 = (bf16[16,4,32,128]{3,2,1,0:T(8,128)(2,1)S(1)}, bf16[16,4,32,128]{3,2,1,0:T(8,128)(2,1)}, u32[]{:S(2)}) copy-start(bf16[16,4,32,128]{3,2,1,0:T(8,128)(2,1)} %get-tuple-element.9) | copy-start | bytes 1572868
  75.9 9.7 %copy-start.18 = (bf16[16,4,32,128]{3,2,1,0:T(8,128)(2,1)S(1)}, bf16[16,4,32,128]{3,2,1,0:T(8,128)(2,1)}, u32[]{:S(2)}) copy-start(bf16[16,4,32,128]{3,2,1,0:T(8,128)(2,1)} %get-tuple-element.10) | copy-start | bytes 1572868
  75.9 10.6 %copy-start.17 = (bf16[16,4,32,128]{3,2,1,0:T(8,128)(2,1)S(1)}, bf16[16,4,32,128]{3,2,1,0:T(8,128)(2,1)}, u32[]{:S(2)}) copy-start(bf16[16,4,32,128]{3,2,1,0:T(8,128)(2,1)} %get-tuple-element.11) | copy-start | bytes 1572868
  77.2 10.2 %copy-start.16 = (bf16[16,4,32,128]{3,2,1,0:T(8,128)(2,1)S(1)}, bf16[16,4,32,128]{3,2,1,0:T(8,128)(2,1)}, u32[]{:S(2)}) copy-start(bf16[16,4,32,128]{3,2,1,0:T(8,128)(2,1)} %get-tuple-element.12) | copy-start | bytes 1572868
  77.2 11.0 %copy-start.15 = (bf16[16,4,32,128]{3,2,1,0:T(8,128)(2,1)S(1)}, bf16[16,4,32,128]{3,2,1,0:T(8,128)(2,1)}, u32[]{:S(2)}) copy-start(bf16[16,4,32,128]{3,2,1,0:T(8,128)(2,1)} %get-tuple-element.13) | copy-start | bytes 1572868
  79.2 9.9 %copy-start.14 = (bf16[16,4,32,128]{3,2,1,0:T(8,128)(2,1)S(1)}, bf16[16,4,32,128]{3,2,1,0:T(8,128)(2,1)}, u32[]{:S(2)}) copy-start(bf16[16,4,32,128]{3,2,1,0:T(8,128)(2,1)} %get-tuple-element.14) | copy-start | bytes 1572868
  81.1 8.7 %copy-start.13 = (bf16[16,4,32,128]{3,2,1,0:T(8,128)(2,1)S(1)}, bf16[16,4,32,128]{3,2,1,0:T(8,128)(2,1)}, u32[]{:S(2)}) copy-start(bf16[16,4,32,128]{3,2,1,0:T(8,128)(2,1)} %get-tuple-element.15) | copy-start | bytes 1572868
  83.1 7.6 %copy-start.12 = (bf16[16,4,32,128]{3,2,1,0:T(8,128)(2,1)S(1)}, bf16[16,4,32,128]{3,2,1,0:T(8,128)(2,1)}, u32[]{:S(2)}) copy-start(bf16[16,4,32,128]{3,2,1,0:T(8,128)(2,1)} %get-tuple-element.16) | copy-start | bytes 1572868
  84.8 7.6 %copy-start.11 = (bf16[16,4,32,128]{3,2,1,0:T(8,128)(2,1)S(1)}, bf16[16,4,32,128]{3,2,1,0:T(8,128)(2,1)}, u32[]{:S(2)}) copy-start(bf16[16,4,32,128]{3,2,1,0:T(8,128)(2,1)} %get-tuple-element.17) | copy-start | bytes 1572868
  89.0 7.6 %copy-start.35 = (bf16[16,4,32,128]{3,2,1,0:T(8,128)(2,1)S(1)}, bf16[16,4,32,128]{3,2,1,0:T(8,128)(2,1)}, u32[]{:S(2)}) copy-start(bf16[16,4,32,128]{3,2,1,0:T(8,128)(2,1)} %get-tuple-element.23) | copy-start | bytes 1572868
  89.9 7.6 %copy-start.34 = (bf16[16,4,32,128]{3,2,1,0:T(8,128)(2,1)S(1)}, bf16[16,4,32,128]{3,2,1,0:T(8,128)(2,1)}, u32[]{:S(2)}) copy-start(bf16[16,4,32,128]{3,2,1,0:T(8,128)(2,1)} %get-tuple-element.24) | copy-start | bytes 1572868
  90.7 7.6 %copy-start.33 = (bf16[16,4,32,128]{3,2,1,0:T(8,128)(2,1)S(1)}, bf16[16,4,32,128]{3,2,1,0:T(8,128)(2,1)}, u32[]{:S(2)}) copy-start(bf16[16,4,32,128]{3,2,1,0:T(8,128)(2,1)} %get-tuple-element.25) | copy-start | bytes 1572868
  91.6 7.6 %copy-start.32 = (bf16[16,4,32,128]{3,2,1,0:T(8,128)(2,1)S(1)}, bf16[16,4,32,128]{3,2,1,0:T(8,128)(2,1)}, u32[]{:S(2)}) copy-start(bf16[16,4,32,128]{3,2,1,0:T(8,128)(2,1)} %get-tuple-element.26) | copy-start | bytes 1572868
  93.3 6.8 %copy-start.31 = (bf16[16,4,32,128]{3,2,1,0:T(8,128)(2,1)S(1)}, bf16[16,4,32,128]{3,2,1,0:T(8,128)(2,1)}, u32[]{:S(2)}) copy-start(bf16[16,4,32,128]{3,2,1,0:T(8,128)(2,1)} %get-tuple-element.27) | copy-start | bytes 1572868
  94.1 6.8 %copy-start.30 = (bf16[16,4,32,128]{3,2,1,0:T(8,128)(2,1)S(1)}, bf16[16,4,32,128]{3,2,1,0:T(8,128)(2,1)}, u32[]{:S(2)}) copy-start(bf16[16,4,32,128]{3,2,1,0:T(8,128)(2,1)} %get-tuple-element.28) | copy-start | bytes 1572868
  95.0 6.8 %copy-start.29 = (bf16[16,4,32,128]{3,2,1,0:T(8,128)(2,1)S(1)}, bf16[16,4,32,128]{3,2,1,0:T(8,128)(2,1)}, u32[]{:S(2)}) copy-start(bf16[16,4,32,128]{3,2,1,0:T(8,128)(2,1)} %get-tuple-element.22) | copy-start | bytes 1572868
  140.3 4.0 %copy-start.1 = (bf16[512,3,3,3,128]{4,0,3,2,1:T(8,128)(2,1)S(1)}, bf16[512,3,3,3,128]{4,0,3,2,1:T(8,128)(2,1)}, u32[]{:S(2)}) copy-start(bf16[512,3,3,3,128]{4,0,3,2,1:T(8,128)(2,1)} %param.7) | copy-start | bytes 10616836
  168.8 6.7 %copy-start.10 = (bf16[16,4,32,128]{3,2,1,0:T(8,128)(2,1)S(1)}, bf16[16,4,32,128]{3,2,1,0:T(8,128)(2,1)}, u32[]{:S(2)}) copy-start(bf16[16,4,32,128]{3,2,1,0:T(8,128)(2,1)} %get-tuple-element.37) | copy-start | bytes 1572868
  168.8 6.9 %copy-start.9 = (bf16[16,4,32,128]{3,2,1,0:T(8,128)(2,1)S(1)}, bf16[16,4,32,128]{3,2,1,0:T(8,128)(2,1)}, u32[]{:S(2)}) copy-start(bf16[16,4,32,128]{3,2,1,0:T(8,128)(2,1)} %get-tuple-element.38) | copy-start | bytes 1572868
  168.8 7.2 %copy-start.8 = (bf16[16,4,32,128]{3,2,1,0:T(8,128)(2,1)S(1)}, bf16[16,4,32,128]{3,2,1,0:T(8,128)(2,1)}, u32[]{:S(2)}) copy-start(bf16[16,4,32,128]{3,2,1,0:T(8,128)(2,1)} %get-tuple-element.39) | copy-start | bytes 1572868
  168.8 7.4 %copy-start.7 = (bf16[16,4,32,128]{3,2,1,0:T(8,128)(2,1)S(1)}, bf16[16,4,32,128]{3,2,1,0:T(8,128)(2,1)}, u32[]{:S(2)}) copy-start(bf16[16,4,32,128]{3,2,1,0:T(8,128)(2,1)} %get-tuple-element.40) | copy-start | bytes 1572868
  168.8 7.7 %copy-start.6 = (bf16[16,4,32,128]{3,2,1,0:T(8,128)(2,1)S(1)}, bf16[16,4,32,128]{3,2,1,0:T(8,128)(2,1)}, u32[]{:S(2)}) copy-start(bf16[16,4,32,128]{3,2,1,0:T(8,128)(2,1)} %get-tuple-element.41) | copy-start | bytes 1572868
  170.3 6.5 %copy-start.5 = (bf16[16,4,32,128]{3,2,1,0:T(8,128)(2,1)S(1)}, bf16[16,4,32,128]{3,2,1,0:T(8,128)(2,1)}, u32[]{:S(2)}) copy-start(bf16[16,4,32,128]{3,2,1,0:T(8,128)(2,1)} %get-tuple-element.42) | copy-start | bytes 1572868
  171.6 5.4 %copy-start.4 = (bf16[16,4,32,128]{3,2,1,0:T(8,128)(2,1)S(1)}, bf16[16,4,32,128]{3,2,1,0:T(8,128)(2,1)}, u32[]{:S(2)}) copy-start(bf16[16,4,32,128]{3,2,1,0:T(8,128)(2,1)} %get-tuple-element.43) | copy-start | bytes 1572868
  172.9 4.3 %copy-start.3 = (bf16[16,4,32,128]{3,2,1,0:T(8,128)(2,1)S(1)}, bf16[16,4,32,128]{3,2,1,0:T(8,128)(2,1)}, u32[]{:S(2)}) copy-start(bf16[16,4,32,128]{3,2,1,0:T(8,128)(2,1)} %get-tuple-element.44) | copy-start | bytes 1572868
  175.5 2.2 %copy-start.2 = (bf16[16,4,32,128]{3,2,1,0:T(8,128)(2,1)S(1)}, bf16[16,4,32,128]{3,2,1,0:T(8,128)(2,1)}, u32[]{:S(2)}) copy-start(bf16[16,4,32,128]{3,2,1,0:T(8,128)(2,1)} %get-tuple-element.45) | copy-start | bytes 1572868
  (9 other events, 19.3 us)
Sparse Core Ops, SparseCore 0:
  68.8 18.9 reduce-scatter.4

commit v2 on v1

v2 whole, which is shorter than its diff:
```python
import functools
import math

import jax
import jax.numpy as jnp
from jax import lax
from jax.experimental import pallas as pl
from jax.experimental.pallas import tpu as pltpu
from jax.sharding import PartitionSpec as P

TAPS = 27
F32 = jnp.float32
BF16 = jnp.bfloat16
NT = (((1,), (1,)), ((), ()))


def kernel(
    cfg, act, grad, pre, w_one, w_two,
    gi, g_one, g_two,
    gall, pall, aall, slab, shifted, cols, wv_one, wv_two,
    send_one, recv_one, send_two, recv_two, part_two, lhs,
    w_sem, ag_s, ag_r, ap_s, ap_r, aa_s, aa_r, r1_s, r1_r, r2_s, r2_r,
):
    n, groups, planes, height, width, chan, factor = cfg
    area = height * width
    local = planes * area
    lanes = grad.shape[1]
    mid = w_two.shape[1]
    me = lax.axis_index("space")
    mine = lax.axis_index("filt")

    def w_copy(src, dst, t, s):
        return pltpu.make_async_copy(
            src.at[t], dst.at[:, pl.ds(t * lanes, lanes)], w_sem.at[s, t]
        )

    for t in range(TAPS):
        w_copy(w_two, wv_two, t, 1).start()

    barrier = pltpu.get_barrier_semaphore()

    def greet_space(k, c):
        pl.semaphore_signal(
            barrier, inc=1, device_id={"space": lax.rem(me + k, n)},
            device_id_type=pl.DeviceIdType.MESH,
        )
        return c

    lax.fori_loop(1, n, greet_space, 0)
    for k in range(1, groups):
        pl.semaphore_signal(
            barrier, inc=1, device_id={"filt": lax.rem(mine + k, groups)},
            device_id_type=pl.DeviceIdType.MESH,
        )
    pl.semaphore_wait(barrier, n + groups - 2)

    def over_space(src, dst, ss, rs, k):
        return pltpu.make_async_remote_copy(
            src_ref=src, dst_ref=dst, send_sem=ss, recv_sem=rs,
            device_id={"space": lax.rem(me + k, n)},
            device_id_type=pl.DeviceIdType.MESH,
        )

    def ag_out(k):
        return over_space(grad, gall.at[me], ag_s.at[k], ag_r.at[k], k)

    def ag_pre(k):
        return over_space(pall.at[me], pall.at[me], ap_s.at[k], ap_r.at[k], k)

    def ex_act(s, k):
        return over_space(
            act.at[s, lax.rem(me + k, n)], aall.at[s, me], aa_s.at[s, k], aa_r.at[s, k], k
        )

    def each(lo, hi, fn):
        def body(k, c):
            fn(k)
            return c

        lax.fori_loop(lo, hi, body, 0)

    ag_out(1).start()
    ag_out(n - 1).start()
    each(2, n - 1, lambda k: ag_out(k).start())
    each(1, n, lambda k: ex_act(0, k).start())
    for t in range(TAPS):
        w_copy(w_one, wv_one, t, 0).start()

    gall[me] = grad[...]
    aall[0, me] = act[0, me]
    aall[1, me] = act[1, me]
    shifted[...] = jnp.zeros_like(shifted)
    zero_plane = jnp.zeros((chan, area), BF16)
    for t in range(9):
        lhs[pl.ds(t * chan, chan), pl.ds(area, area)] = zero_plane
        lhs[pl.ds((18 + t) * chan, chan), pl.ds(n * planes * area, area)] = zero_plane

    def build_cols(field):
        below = field[lax.rem(me + n - 1, n), pl.ds(local - area, area), :]
        above = field[lax.rem(me + 1, n), pl.ds(0, area), :]
        slab[pl.ds(0, area), :] = jnp.where(me > 0, below.astype(F32), 0.0)
        slab[pl.ds(area, local), :] = field[me].astype(F32)
        slab[pl.ds(area + local, area), :] = jnp.where(me < n - 1, above.astype(F32), 0.0)
        whole = slab[...]
        rows = whole.shape[0]
        col = lax.rem(lax.broadcasted_iota(jnp.int32, whole.shape, 0), width)
        for c in range(3):
            moved = whole if c == 1 else pltpu.roll(whole, (c - 1) % rows, 0)
            if c == 0:
                moved = jnp.where(col < width - 1, moved, 0.0)
            if c == 2:
                moved = jnp.where(col > 0, moved, 0.0)
            shifted[c, :, pl.ds(1, height), :, :] = moved.astype(BF16).reshape(
                planes + 2, height, width, lanes
            )
        t = 0
        for a in range(3):
            for b in range(3):
                for c in range(3):
                    window = shifted[c, pl.ds(2 - a, planes), pl.ds(2 - b, height), :, :]
                    cols[:, pl.ds(t * lanes, lanes)] = window.reshape(local, lanes)
                    t += 1

    def build_lhs(s):
        lane = lax.broadcasted_iota(jnp.int32, (chan, local), 1)
        row = lax.rem(lane, area) // width
        col = lax.rem(lane, width)

        def body(j, carry):
            block = aall[s, j].astype(F32)
            for b in range(3):
                for c in range(3):
                    step = (b - 1) * width + (c - 1)
                    moved = block if step == 0 else pltpu.roll(block, (-step) % local, 1)
                    keep = None
                    if b != 1:
                        keep = (row > 0) if b == 0 else (row < height - 1)
                    if c != 1:
                        other = (col > 0) if c == 0 else (col < width - 1)
                        keep = other if keep is None else keep & other
                    if keep is not None:
                        moved = jnp.where(keep, moved, 0.0)
                    moved = moved.astype(BF16)
                    for a in range(3):
                        t = (a * 3 + b) * 3 + c
                        start = pl.multiple_of((j * planes + 2 - a) * area, area)
                        lhs[pl.ds(t * chan, chan), pl.ds(start, local)] = moved
            return carry

        lax.fori_loop(0, n, body, 0)

    def filter_grad(field, out):
        out[...] = jnp.zeros_like(out)

        def body(j, carry):
            start = pl.multiple_of((j * planes + 1) * area, area)
            out[...] += jnp.dot(
                lhs[:, pl.ds(start, local)], field[j], preferred_element_type=F32
            )
            return carry

        lax.fori_loop(0, n, body, 0)
        out[...] = out[...] * factor

    def over_filt(src, dst, ss, rs, k):
        return pltpu.make_async_remote_copy(
            src_ref=src, dst_ref=dst, send_sem=ss, recv_sem=rs,
            device_id={"filt": lax.rem(mine + k, groups)},
            device_id_type=pl.DeviceIdType.MESH,
        )

    def rs_one(k):
        return over_filt(
            send_one.at[k - 1], recv_one.at[k - 1], r1_s.at[k - 1], r1_r.at[k - 1], k
        )

    def rs_two(k):
        return over_filt(
            send_two.at[lax.rem(mine + k, groups)], recv_two.at[k - 1],
            r2_s.at[k - 1], r2_r.at[k - 1], k,
        )

    ag_out(1).wait_recv()
    ag_out(n - 1).wait_recv()
    build_cols(gall)
    for t in range(TAPS):
        w_copy(w_two, wv_two, t, 1).wait()
    share = mid // groups

    def hidden(group):
        start = pl.multiple_of(group * share, share)
        return lax.dot_general(
            cols[...], wv_two[pl.ds(start, share), :], NT, preferred_element_type=F32
        )

    for k in range(1, groups):
        send_one[k - 1] = hidden(lax.rem(mine + k, groups)).astype(BF16)
        rs_one(k).start()
    total = hidden(mine)
    for k in range(1, groups):
        rs_one(k).wait_recv()
        total = total + recv_one[k - 1].astype(F32)
    pall[me] = jnp.where(pre[...].astype(F32) > 0, total, 0.0).astype(BF16)
    ag_pre(1).start()
    ag_pre(n - 1).start()
    each(2, n - 1, lambda k: ag_pre(k).start())
    each(1, n, lambda k: ex_act(1, k).start())

    each(1, n, lambda k: ex_act(0, k).wait_recv())
    build_lhs(0)
    each(2, n - 1, lambda k: ag_out(k).wait_recv())
    filter_grad(gall, g_two)

    ag_pre(1).wait_recv()
    ag_pre(n - 1).wait_recv()
    build_cols(pall)
    for t in range(TAPS):
        w_copy(w_one, wv_one, t, 0).wait()
    rows = height // groups
    in_chan = w_one.shape[1]
    for q in range(in_chan // 128):
        piece = lax.dot_general(
            cols[...], wv_one[pl.ds(q * 128, 128), :], NT, preferred_element_type=F32
        ).reshape(planes, groups, rows * width, 128)
        for f in range(groups):
            for p in range(planes):
                part_two[f, pl.ds(p * rows * width, rows * width), pl.ds(q * 128, 128)] = piece[p, f]
    send_two[...] = part_two[...].astype(BF16)
    for k in range(1, groups):
        rs_two(k).start()

    each(1, n, lambda k: ex_act(1, k).wait_recv())
    build_lhs(1)
    each(2, n - 1, lambda k: ag_pre(k).wait_recv())
    filter_grad(pall, g_one)

    result = part_two[mine]
    for k in range(1, groups):
        rs_two(k).wait_recv()
        result = result + recv_two[k - 1].astype(F32)
    gi[...] = result.astype(BF16)

    for k in range(1, groups):
        rs_one(k).wait_send()
        rs_two(k).wait_send()

    def drain(k):
        ag_out(k).wait_send()
        ag_pre(k).wait_send()
        ex_act(0, k).wait_send()
        ex_act(1, k).wait_send()

    each(1, n, drain)


def shards(inputs, pre_hidden, weight_one, weight_two, grad_out):
    planes, height, width, in_chan = inputs.shape
    mid = pre_hidden.shape[3]
    lanes = grad_out.shape[3]
    n = lax.axis_size("space")
    groups = lax.axis_size("filt")
    area = height * width
    local = planes * area
    factor = 1.0 / math.sqrt(local * n)
    own = in_chan // n
    chan = max(own, 16)

    activity = jnp.maximum(pre_hidden, jnp.zeros_like(pre_hidden))
    act = jnp.stack([activity.reshape(local, mid), inputs.reshape(local, in_chan)])
    act = jnp.swapaxes(act, 1, 2).reshape(2, n, own, local)
    if chan != own:
        act = jnp.pad(act, ((0, 0), (0, 0), (0, chan - own), (0, 0)))
    share = mid // groups
    pre = lax.dynamic_slice_in_dim(
        pre_hidden.reshape(local, mid), lax.axis_index("filt") * share, share, 1
    )

    def tap_major(weight):
        return jnp.transpose(weight, (1, 2, 3, 0, 4)).reshape(TAPS, weight.shape[0], lanes)

    out_rows = planes * (height // groups) * width
    vmem = pl.BlockSpec(memory_space=pltpu.VMEM)
    hbm = pl.BlockSpec(memory_space=pl.ANY)
    dma = pltpu.SemaphoreType.DMA
    cfg = (n, groups, planes, height, width, chan, factor)
    gi, g_one, g_two = pl.pallas_call(
        functools.partial(kernel, cfg),
        out_shape=(
            jax.ShapeDtypeStruct((out_rows, in_chan), BF16),
            jax.ShapeDtypeStruct((TAPS * chan, lanes), F32),
            jax.ShapeDtypeStruct((TAPS * chan, lanes), F32),
        ),
        in_specs=[vmem, vmem, vmem, hbm, hbm],
        out_specs=(vmem, vmem, vmem),
        scratch_shapes=[
            pltpu.VMEM((n, local, lanes), BF16),
            pltpu.VMEM((n, local, lanes), BF16),
            pltpu.VMEM((2, n, chan, local), BF16),
            pltpu.VMEM((local + 2 * area, lanes), F32),
            pltpu.VMEM((3, planes + 2, height + 2, width, lanes), BF16),
            pltpu.VMEM((local, TAPS * lanes), BF16),
            pltpu.VMEM((in_chan, TAPS * lanes), BF16),
            pltpu.VMEM((mid, TAPS * lanes), BF16),
            pltpu.VMEM((groups - 1, local, share), BF16),
            pltpu.VMEM((groups - 1, local, share), BF16),
            pltpu.VMEM((groups, out_rows, in_chan), BF16),
            pltpu.VMEM((groups - 1, out_rows, in_chan), BF16),
            pltpu.VMEM((groups, out_rows, in_chan), F32),
            pltpu.VMEM((TAPS * chan, (n * planes + 2) * area), BF16),
            dma((2, TAPS)),
            dma((n,)), dma((n,)), dma((n,)), dma((n,)),
            dma((2, n)), dma((2, n)),
            dma((groups - 1,)), dma((groups - 1,)),
            dma((groups - 1,)), dma((groups - 1,)),
        ],
        compiler_params=pltpu.CompilerParams(
            collective_id=0, has_side_effects=True, vmem_limit_bytes=60 * 1024 * 1024
        ),
    )(act, grad_out.reshape(local, lanes), pre, tap_major(weight_one), tap_major(weight_two))

    def filters(g):
        g = g.reshape(3, 3, 3, chan, lanes)[:, :, :, :own, :]
        return jnp.transpose(g, (3, 0, 1, 2, 4))

    return gi.reshape(planes, height // groups, width, in_chan), filters(g_one), filters(g_two)


def solution(mesh):
    placed = (
        P("space", None, None, None),
        P("space", None, None, None),
        P(None, None, None, None, "filt"),
        P(None, None, None, None, "filt"),
        P("space", None, None, "filt"),
    )
    return jax.shard_map(
        shards,
        mesh=mesh,
        in_specs=placed,
        out_specs=(
            P("space", "filt", None, None),
            P("space", None, None, None, "filt"),
            P("space", None, None, None, "filt"),
        ),
        check_vma=False,
    )
```

time: 191 us -> 59.7 us (0.31)
  blocking collectives: 87.4 us -> 0 us
  matrix products: 55.3 us -> 0 us
  Pallas kernels: 0 us -> 48.4 us
  between operations: 15 us -> 0.66 us
  local copies, waits for them, and re-layouts: 21.9 us -> 8.51 us
  starting transfers between devices: 7.32 us -> 0 us
    all_gather x2 -> x0, blocking collectives: 70 us -> none  [the longest x1 38.5 us: shards(): out_all = pad_all(lax.all_gather(grad_out, 'space', axis=0, tiled=True))]
    dot_general x108 -> x0, matrix products: 55.3 us -> none  [the longest x54 37.7 us: weight_terms(): lax.dot_general(source, window, (((1,), (0,)), ((), ())), preferred_eleme...]
    pallas_call x0 -> x1, Pallas kernels: none -> 48.4 us  [shards(): pl.pallas_call(functools.partial(kernel, cfg), out_shape=(jax.ShapeDtypeS...]
    slice x9 -> x0, local copies, waits for them, and re-layouts: 18 us -> none  [the longest x8 16.7 us: window_at(): padded[2 - tap[0]:2 - tap[0] + planes, 2 - tap[1]:2 - tap[1] + height, 2...]
    unnamed x1 -> x0, blocking collectives: 17.4 us -> none
    all_to_all x1 -> x0, starting transfers between devices: 7.28 us -> none  [shards(): both = lax.all_to_all(both, 'space', 1, 1)]
    unnamed x81 -> x3, local copies, waits for them, and re-layouts: 0.79 us -> 5.82 us
    convert_element_type x1 -> x0, local copies, waits for them, and re-layouts: 2.09 us -> none  [shards(): grad_inputs = grad_rows.astype(jnp.bfloat16)]
  transfers between devices with their start and end apart: 2 -> 0, of which waited for: 0 -> 0; matrix products, arithmetic and copies ran while one was open for 25% -> 0% of each run, Pallas kernels for 0% -> 0%
where the time goes in v2:
time: 59.7 us; the launch traced here: 59.4 us
  Pallas kernels  48.4 us (81%)
  local copies, waits for them, and re-layouts  8.51 us (14%)
  other arithmetic  1.81 us (3%)
  between operations  0.66 us (1%)
    pallas_call x1, Pallas kernels, shards(): pl.pallas_call(functools.partial(kernel, cfg), out_shape=(jax.ShapeDtypeS...  48.4 us
    unnamed x3, local copies, waits for them, and re-layouts  5.82 us
    dynamic_slice x1, local copies, waits for them, and re-layouts, shards(): lax.dynamic_slice_in_dim(pre_hidden.reshape(local, mid), lax.axis_index('...  1.48 us
    another operation x2, local copies, waits for them, and re-layouts, shards(): jnp.stack([activity.reshape(local, mid), inputs.reshape(local, in_chan)])  1.21 us

profile of v2, /device:TPU:0, one launch (start us, length us, event | category | flops | bytes accessed | tf_op | source)
XLA Modules:
  0.0 59.4 jit_solution(11077661781231178431)
XLA Ops:
  0.6 1.5 %constant_dynamic-slice_fusion.pre = bf16[256,128]{1,0:T(8,128)(2,1)} fusion(bf16[256,512]{1,0:T(8,128)(2,1)} %bitcast.28, s32[]{:T(128)S(6)} %select_n.3), kind=kLoop, calls=%fused_computation.2 | loop fusion | bytes 131076 | tf_op jit(solution)/shard_map/dynamic_slice | solution.py:274
  2.1 1.1 %copy.9 = bf16[1,256,512]{1,2,0:T(8,128)(2,1)S(1)} copy(bf16[1,256,512]{2,1,0:T(8,128)(2,1)} %bitcast.29) | data formatting | bytes 524288 | tf_op jit(solution)/shard_map/stack;reshape | solution.py:269
  3.2 1.0 %broadcast_maximum_fusion = bf16[2,4,32,512]{3,2,1,0:T(8,128)(2,1)S(1)} fusion(bf16[2,4,32,512]{3,2,1,0:T(8,128)(2,1)} %param.6), kind=kLoop, calls=%fused_computation.1 | loop fusion | flops 131072 | bytes 524288 | tf_op jit(solution)/shard_map/max | solution.py:268
  4.2 0.1 copy.8
  4.3 0.8 %pad_maximum_fusion = bf16[2,256,512]{1,2,0:T(8,128)(2,1)} fusion(bf16[1,256,512]{1,2,0:T(8,128)(2,1)S(1)} %copy.9, bf16[1,256,512]{1,2,0:T(8,128)(2,1)S(1)} %copy.8), kind=kLoop, calls=%fused_computation | loop fusion | flops 262144 | bytes 1048576 | tf_op jit(solution)/shard_map/stack | solution.py:269
  5.2 48.4 %shard_map.76 = (bf16[64,512]{1,0:T(8,128)(2,1)}, f32[1728,128]{1,0:T(8,128)}, f32[1728,128]{1,0:T(8,128)}) custom-call(bf16[2,8,64,256]{3,2,1,0:T(8,128)(2,1)} %bitcast.24, bf16[256,128]{1,0:T(8,128)(2,1)} %bitcast.30, bf16[256,128]{1,0:T(8,128)(2,1)} %constant_dynamic-slice_fusion.pre, bf16[27,512,128]{2,1,0:T(8,128)(2,1)} %bitcast.22, ...), custom_call_target="tpu_custom_call" | custom-call | tf_op jit(solution)/shard_map/pallas_call | solution.py:286
  53.5 1.5 %copy.14 = bf16[2,1,32,512]{3,2,1,0:T(8,128)(2,1)} copy(bf16[2,1,32,512]{3,2,1,0:T(8,128)(2,1)} %bitcast.31) | data formatting | bytes 131072
  55.0 2.2 %copy.15 = f32[64,3,3,3,128]{4,0,3,2,1:T(8,128)} copy(f32[64,3,3,3,128]{4,0,3,2,1:T(8,128)} %bitcast.27) | data formatting | bytes 1769472
  57.2 2.2 %copy.16 = f32[64,3,3,3,128]{4,0,3,2,1:T(8,128)} copy(f32[64,3,3,3,128]{4,0,3,2,1:T(8,128)} %bitcast.26) | data formatting | bytes 1769472

commit v3 on v2

--- a/solution.py
+++ b/solution.py
@@ -15,13 +15,13 @@
 
 
 def kernel(
-    cfg, act, grad, pre, w_one, w_two,
+    cfg, source, hidden_in, grad, w_one, w_two,
     gi, g_one, g_two,
-    gall, pall, aall, slab, shifted, cols, wv_one, wv_two,
+    act, gall, pall, aall, slab, shifted, cols, wv_one, wv_two,
     send_one, recv_one, send_two, recv_two, part_two, lhs,
     w_sem, ag_s, ag_r, ap_s, ap_r, aa_s, aa_r, r1_s, r1_r, r2_s, r2_r,
 ):
-    n, groups, planes, height, width, chan, factor = cfg
+    n, groups, planes, height, width, chan, own = cfg
     area = height * width
     local = planes * area
     lanes = grad.shape[1]
@@ -61,11 +61,55 @@
             device_id_type=pl.DeviceIdType.MESH,
         )
 
-    def ag_out(k):
-        return over_space(grad, gall.at[me], ag_s.at[k], ag_r.at[k], k)
-
-    def ag_pre(k):
-        return over_space(pall.at[me], pall.at[me], ap_s.at[k], ap_r.at[k], k)
+    partner = me + 1 - 2 * lax.rem(me, 2)
+    evens = list(dict.fromkeys([2, n - 2] + list(range(4, n - 2, 2))))
+
+    def origin(k):
+        return lax.rem(me + n - k, n)
+
+    def to_partner(src, dst, ss, rs):
+        return pltpu.make_async_remote_copy(
+            src_ref=src, dst_ref=dst, send_sem=ss, recv_sem=rs,
+            device_id={"space": partner}, device_id_type=pl.DeviceIdType.MESH,
+        )
+
+    def gather(block, field, ss, rs):
+        def direct(k):
+            return over_space(block, field.at[me], ss.at[k], rs.at[me], k)
+
+        def swap():
+            return to_partner(block, field.at[me], ss.at[1], rs.at[me])
+
+        def forward(k):
+            j = origin(k)
+            return to_partner(field.at[j], field.at[j], ss.at[k + 1], rs.at[j])
+
+        def arrived(k):
+            j = origin(k)
+            to_partner(field.at[j], field.at[j], ss.at[0], rs.at[j]).wait_recv()
+
+        def start():
+            for k in evens[:2]:
+                direct(k).start()
+            swap().start()
+            for k in evens[2:]:
+                direct(k).start()
+
+        def relay():
+            for k in evens:
+                arrived(k)
+                forward(k).start()
+
+        def finish():
+            swap().wait_send()
+            for k in evens:
+                direct(k).wait_send()
+                forward(k).wait_send()
+
+        return start, relay, arrived, finish
+
+    ag_start, ag_relay, ag_arrived, ag_finish = gather(grad, gall, ag_s, ag_r)
+    ap_start, ap_relay, ap_arrived, ap_finish = gather(pall.at[me], pall, ap_s, ap_r)
 
     def ex_act(s, k):
         return over_space(
@@ -79,14 +123,22 @@
 
         lax.fori_loop(lo, hi, body, 0)
 
-    ag_out(1).start()
-    ag_out(n - 1).start()
-    each(2, n - 1, lambda k: ag_out(k).start())
-    each(1, n, lambda k: ex_act(0, k).start())
+    ag_start()
     for t in range(TAPS):
         w_copy(w_one, wv_one, t, 0).start()
 
     gall[me] = grad[...]
+    if chan != own:
+        act[...] = jnp.zeros_like(act)
+    for s, ref in enumerate((hidden_in, source)):
+        wide = ref[...].astype(F32)
+        if s == 0:
+            wide = jnp.maximum(wide, 0.0)
+        wide = wide.T
+        for j in range(n):
+            act[s, j, pl.ds(0, own), :] = wide[j * own : (j + 1) * own].astype(BF16)
+    ag_relay()
+    each(1, n, lambda k: ex_act(0, k).start())
     aall[0, me] = act[0, me]
     aall[1, me] = act[1, me]
     shifted[...] = jnp.zeros_like(shifted)
@@ -160,7 +212,6 @@
             return carry
 
         lax.fori_loop(0, n, body, 0)
-        out[...] = out[...] * factor
 
     def over_filt(src, dst, ss, rs, k):
         return pltpu.make_async_remote_copy(
@@ -180,8 +231,8 @@
             r2_s.at[k - 1], r2_r.at[k - 1], k,
         )
 
-    ag_out(1).wait_recv()
-    ag_out(n - 1).wait_recv()
+    ag_arrived(1)
+    ag_arrived(n - 1)
     build_cols(gall)
     for t in range(TAPS):
         w_copy(w_two, wv_two, t, 1).wait()
@@ -200,19 +251,20 @@
     for k in range(1, groups):
         rs_one(k).wait_recv()
         total = total + recv_one[k - 1].astype(F32)
-    pall[me] = jnp.where(pre[...].astype(F32) > 0, total, 0.0).astype(BF16)
-    ag_pre(1).start()
-    ag_pre(n - 1).start()
-    each(2, n - 1, lambda k: ag_pre(k).start())
-    each(1, n, lambda k: ex_act(1, k).start())
+    own_pre = hidden_in[:, pl.ds(pl.multiple_of(mine * share, share), share)]
+    pall[me] = jnp.where(own_pre.astype(F32) > 0, total, 0.0).astype(BF16)
+    ap_start()
 
     each(1, n, lambda k: ex_act(0, k).wait_recv())
     build_lhs(0)
-    each(2, n - 1, lambda k: ag_out(k).wait_recv())
+    ap_relay()
+    each(1, n, lambda k: ex_act(1, k).start())
+    for k in range(3, n - 2, 2):
+        ag_arrived(k)
     filter_grad(gall, g_two)
 
-    ag_pre(1).wait_recv()
-    ag_pre(n - 1).wait_recv()
+    ap_arrived(1)
+    ap_arrived(n - 1)
     build_cols(pall)
     for t in range(TAPS):
         w_copy(w_one, wv_one, t, 0).wait()
@@ -231,7 +283,8 @@
 
     each(1, n, lambda k: ex_act(1, k).wait_recv())
     build_lhs(1)
-    each(2, n - 1, lambda k: ag_pre(k).wait_recv())
+    for k in range(3, n - 2, 2):
+        ap_arrived(k)
     filter_grad(pall, g_one)
 
     result = part_two[mine]
@@ -245,12 +298,12 @@
         rs_two(k).wait_send()
 
     def drain(k):
-        ag_out(k).wait_send()
-        ag_pre(k).wait_send()
         ex_act(0, k).wait_send()
         ex_act(1, k).wait_send()
 
     each(1, n, drain)
+    ag_finish()
+    ap_finish()
 
 
 def shards(inputs, pre_hidden, weight_one, weight_two, grad_out):
@@ -265,15 +318,7 @@
     own = in_chan // n
     chan = max(own, 16)
 
-    activity = jnp.maximum(pre_hidden, jnp.zeros_like(pre_hidden))
-    act = jnp.stack([activity.reshape(local, mid), inputs.reshape(local, in_chan)])
-    act = jnp.swapaxes(act, 1, 2).reshape(2, n, own, local)
-    if chan != own:
-        act = jnp.pad(act, ((0, 0), (0, 0), (0, chan - own), (0, 0)))
     share = mid // groups
-    pre = lax.dynamic_slice_in_dim(
-        pre_hidden.reshape(local, mid), lax.axis_index("filt") * share, share, 1
-    )
 
     def tap_major(weight):
         return jnp.transpose(weight, (1, 2, 3, 0, 4)).reshape(TAPS, weight.shape[0], lanes)
@@ -282,7 +327,7 @@
     vmem = pl.BlockSpec(memory_space=pltpu.VMEM)
     hbm = pl.BlockSpec(memory_space=pl.ANY)
     dma = pltpu.SemaphoreType.DMA
-    cfg = (n, groups, planes, height, width, chan, factor)
+    cfg = (n, groups, planes, height, width, chan, own)
     gi, g_one, g_two = pl.pallas_call(
         functools.partial(kernel, cfg),
         out_shape=(
@@ -293,6 +338,7 @@
         in_specs=[vmem, vmem, vmem, hbm, hbm],
         out_specs=(vmem, vmem, vmem),
         scratch_shapes=[
+            pltpu.VMEM((2, n, chan, local), BF16),
             pltpu.VMEM((n, local, lanes), BF16),
             pltpu.VMEM((n, local, lanes), BF16),
             pltpu.VMEM((2, n, chan, local), BF16),
@@ -316,10 +362,13 @@
         compiler_params=pltpu.CompilerParams(
             collective_id=0, has_side_effects=True, vmem_limit_bytes=60 * 1024 * 1024
         ),
-    )(act, grad_out.reshape(local, lanes), pre, tap_major(weight_one), tap_major(weight_two))
+    )(
+        inputs.reshape(local, in_chan), pre_hidden.reshape(local, mid),
+        grad_out.reshape(local, lanes), tap_major(weight_one), tap_major(weight_two),
+    )
 
     def filters(g):
-        g = g.reshape(3, 3, 3, chan, lanes)[:, :, :, :own, :]
+        g = (g * factor).reshape(3, 3, 3, chan, lanes)[:, :, :, :own, :]
         return jnp.transpose(g, (3, 0, 1, 2, 4))
 
     return gi.reshape(planes, height // groups, width, in_chan), filters(g_one), filters(g_two)

time: 59.7 us -> 48.9 us (0.82)
  local copies, waits for them, and re-layouts: 8.51 us -> 0.63 us
  Pallas kernels: 48.4 us -> 44.6 us
  other arithmetic: 1.81 us -> 2.82 us
    unnamed x3, local copies, waits for them, and re-layouts: 5.82 us -> 0.63 us
    pallas_call x1, Pallas kernels: 48.4 us -> 44.6 us  [shards(): pl.pallas_call(functools.partial(kernel, cfg), out_shape=(jax.ShapeDtypeS...]
    mul x0 -> x1, other arithmetic: none -> 2.82 us  [filters(): g = (g * factor).reshape(3, 3, 3, chan, lanes)[:, :, :, :own, :]]
    dynamic_slice x1 -> x0, local copies, waits for them, and re-layouts: 1.48 us -> none  [shards(): lax.dynamic_slice_in_dim(pre_hidden.reshape(local, mid), lax.axis_index('...]
    another operation x2 -> x0, local copies, waits for them, and re-layouts: 1.21 us -> none  [shards(): jnp.stack([activity.reshape(local, mid), inputs.reshape(local, in_chan)])]
    max x1 -> x0, other arithmetic: 0.97 us -> none  [shards(): activity = jnp.maximum(pre_hidden, jnp.zeros_like(pre_hidden))]
    another operation x1 -> x0, other arithmetic: 0.84 us -> none  [shards(): jnp.stack([activity.reshape(local, mid), inputs.reshape(local, in_chan)])]
where the time goes in v3:
time: 48.9 us; the launch traced here: 48.7 us
  Pallas kernels  44.6 us (91%)
  other arithmetic  2.82 us (6%)
  between operations  0.65 us (1%)
  local copies, waits for them, and re-layouts  0.63 us (1%)
    pallas_call x1, Pallas kernels, shards(): pl.pallas_call(functools.partial(kernel, cfg), out_shape=(jax.ShapeDtypeS...  44.6 us
    mul x1, other arithmetic, filters(): g = (g * factor).reshape(3, 3, 3, chan, lanes)[:, :, :, :own, :]  2.82 us

profile of v3, /device:TPU:0, one launch (start us, length us, event | category | flops | bytes accessed | tf_op | source)
XLA Modules:
  0.0 48.7 jit_solution(11875601477235917433)
XLA Ops:
  0.6 44.6 %shard_map.76 = (bf16[64,512]{1,0:T(8,128)(2,1)}, f32[1728,128]{1,0:T(8,128)}, f32[1728,128]{1,0:T(8,128)}) custom-call(bf16[256,512]{1,0:T(8,128)(2,1)} %bitcast.22, bf16[256,512]{1,0:T(8,128)(2,1)} %bitcast.23, bf16[256,128]{1,0:T(8,128)(2,1)} %bitcast.24, bf16[27,512,128]{2,1,0:T(8,128)(2,1)} %bitcast.18, bf16[27,512,128]{2,1,0:T(8,128)(2,1)} %bitcast.19), custom_call_target="tpu_custom_call" | custom-call | tf_op jit(solution)/shard_map/pallas_call | solution.py:331
  45.2 0.0 copy-start
  45.3 2.8 %broadcast_multiply_fusion = (f32[1728,128]{1,0:T(8,128)}, f32[1728,128]{1,0:T(8,128)}) fusion(f32[1728,128]{1,0:T(8,128)} %get-tuple-element.8, f32[1728,128]{1,0:T(8,128)} %get-tuple-element.7), kind=kLoop, calls=%fused_computation | loop fusion | flops 442368 | bytes 3538944 | tf_op jit(solution)/shard_map/mul | solution.py:371
  48.1 0.0 copy-done
  48.1 0.6 %copy.10 = bf16[2,1,32,512]{3,2,1,0:T(8,128)(2,1)} copy(bf16[2,1,32,512]{3,2,1,0:T(8,128)(2,1)S(1)} %bitcast.25) | data formatting | bytes 131072
Async XLA Ops:
  45.2 2.8 %copy-start = (bf16[64,512]{1,0:T(8,128)(2,1)S(1)}, bf16[64,512]{1,0:T(8,128)(2,1)}, u32[]{:S(2)}) copy-start(bf16[64,512]{1,0:T(8,128)(2,1)} %get-tuple-element.6) | copy-start | bytes 196612

commit v4 on v3

--- a/solution.py
+++ b/solution.py
@@ -248,6 +248,8 @@
         send_one[k - 1] = hidden(lax.rem(mine + k, groups)).astype(BF16)
         rs_one(k).start()
     total = hidden(mine)
+    each(1, n, lambda k: ex_act(0, k).wait_recv())
+    build_lhs(0)
     for k in range(1, groups):
         rs_one(k).wait_recv()
         total = total + recv_one[k - 1].astype(F32)
@@ -255,13 +257,11 @@
     pall[me] = jnp.where(own_pre.astype(F32) > 0, total, 0.0).astype(BF16)
     ap_start()
 
-    each(1, n, lambda k: ex_act(0, k).wait_recv())
-    build_lhs(0)
-    ap_relay()
-    each(1, n, lambda k: ex_act(1, k).start())
     for k in range(3, n - 2, 2):
         ag_arrived(k)
     filter_grad(gall, g_two)
+    ap_relay()
+    each(1, n, lambda k: ex_act(1, k).start())
 
     ap_arrived(1)
     ap_arrived(n - 1)

time: 48.9 us -> 48.8 us (level)
  no operation moved by 1% of the time
where the time goes in v4:
time: 48.8 us; the launch traced here: 48.7 us
  Pallas kernels  44.6 us (91%)
  other arithmetic  2.82 us (6%)
  between operations  0.65 us (1%)
  local copies, waits for them, and re-layouts  0.63 us (1%)
    pallas_call x1, Pallas kernels, shards(): pl.pallas_call(functools.partial(kernel, cfg), out_shape=(jax.ShapeDtypeS...  44.6 us
    mul x1, other arithmetic, filters(): g = (g * factor).reshape(3, 3, 3, chan, lanes)[:, :, :, :own, :]  2.82 us

profile of v4, /device:TPU:0, one launch (start us, length us, event | category | flops | bytes accessed | tf_op | source)
XLA Modules:
  0.0 48.7 jit_solution(5985020823870064735)
XLA Ops:
  0.6 44.6 %shard_map.76 = (bf16[64,512]{1,0:T(8,128)(2,1)}, f32[1728,128]{1,0:T(8,128)}, f32[1728,128]{1,0:T(8,128)}) custom-call(bf16[256,512]{1,0:T(8,128)(2,1)} %bitcast.22, bf16[256,512]{1,0:T(8,128)(2,1)} %bitcast.23, bf16[256,128]{1,0:T(8,128)(2,1)} %bitcast.24, bf16[27,512,128]{2,1,0:T(8,128)(2,1)} %bitcast.18, bf16[27,512,128]{2,1,0:T(8,128)(2,1)} %bitcast.19), custom_call_target="tpu_custom_call" | custom-call | tf_op jit(solution)/shard_map/pallas_call | solution.py:331
  45.2 0.0 copy-start
  45.2 2.8 %broadcast_multiply_fusion = (f32[1728,128]{1,0:T(8,128)}, f32[1728,128]{1,0:T(8,128)}) fusion(f32[1728,128]{1,0:T(8,128)} %get-tuple-element.8, f32[1728,128]{1,0:T(8,128)} %get-tuple-element.7), kind=kLoop, calls=%fused_computation | loop fusion | flops 442368 | bytes 3538944 | tf_op jit(solution)/shard_map/mul | solution.py:371
  48.0 0.0 copy-done
  48.0 0.6 %copy.10 = bf16[2,1,32,512]{3,2,1,0:T(8,128)(2,1)} copy(bf16[2,1,32,512]{3,2,1,0:T(8,128)(2,1)S(1)} %bitcast.25) | data formatting | bytes 131072
Async XLA Ops:
  45.2 2.8 %copy-start = (bf16[64,512]{1,0:T(8,128)(2,1)S(1)}, bf16[64,512]{1,0:T(8,128)(2,1)}, u32[]{:S(2)}) copy-start(bf16[64,512]{1,0:T(8,128)(2,1)} %get-tuple-element.6) | copy-start | bytes 196612
